TPU v7x, 256 devices: a whole 4x4x8 slice. The times are simulated.
256 devices in a mesh: dp: 32 (over x_hi, z, core), section: 8 (over y, x_lo).
Axes of the slice: x: 4 (x_hi: 2, x_lo: 2; x = x_hi * 2 + x_lo), y: 4, z: 8, core: 2. Of those that a mesh axis runs over, the one named last changes fastest.
Arguments:
- hidden: bfloat16 [6144, 5120], P('dp', 'section'), may hold values from -450 to 450
- norm_gain: float32 [5120], P('section'), may hold values from 0.5 to 1.5
- kv_weight: bfloat16 [5120, 1024], P('section'), may hold values from -0.078125 to 0.078125
- queries: bfloat16 [6144, 20480], P('dp', 'section'), may hold values from -150 to 150
- out_grad: bfloat16 [6144, 20480], P('dp', 'section'), may hold values from -6 to 6
Outputs:
- query_grad: bfloat16 [6144, 20480], P('dp', 'section')
- kv_weight_grad: float32 [5120, 1024], P('section')
- gain_grad: float32 [5120], P('section')
- normed_grad: bfloat16 [6144, 5120], P('dp', 'section')
All inputs are finite; a program needn't handle non-finite values.
Results may differ from a plain program's by a relative error of at most 0.015.
The roundings to bfloat16 on the way count: a program that leaves them out, or rounds other values in their place, can miss the bound.
Values may be sent and summed in bfloat16 or wider, within the bound.
A program may use at most 64 MiB of HBM per device.

v0:
```python
import jax
import jax.numpy as jnp
from jax import lax
from jax.sharding import PartitionSpec as P

D = 5120
HD = 128
KVH = 4
QH = 20


EPSILON = 1e-05


def attend(query_layer, key_rows, value_rows, grad_layer):
    tok_rows = query_layer.shape[0]
    group_size = QH // KVH
    score_scale = HD ** (-0.5)
    query_pos = lax.broadcasted_iota(jnp.int32, (tok_rows, tok_rows), 0)
    key_pos = lax.broadcasted_iota(jnp.int32, (tok_rows, tok_rows), 1)
    causal = key_pos <= query_pos
    query_parts = []
    key_parts = []
    value_parts = []
    for kv_head in range(KVH):
        first_col = kv_head * group_size * HD
        last_col = first_col + group_size * HD
        q_block = query_layer[:, first_col:last_col].reshape(tok_rows, group_size, HD)
        g_block = grad_layer[:, first_col:last_col].reshape(tok_rows, group_size, HD)
        k_block = key_rows[:, kv_head * HD : (kv_head + 1) * HD]
        v_block = value_rows[:, kv_head * HD : (kv_head + 1) * HD]
        scores = (
            jnp.einsum("qhd,kd->hqk", q_block, k_block, preferred_element_type=jnp.float32)
            * score_scale
        )
        scores = jnp.where(causal[None], scores, -1e30)
        row_max = jnp.max(scores, axis=2, keepdims=True)
        weights = jnp.exp(scores - row_max)
        attn_prob = weights / jnp.sum(weights, axis=2, keepdims=True)
        prob_low = attn_prob.astype(jnp.bfloat16)
        value_parts.append(
            jnp.einsum("hqk,qhd->kd", prob_low, g_block, preferred_element_type=jnp.float32)
        )
        prob_grad = jnp.einsum("qhd,kd->hqk", g_block, v_block, preferred_element_type=jnp.float32)
        row_inner = jnp.sum(attn_prob * prob_grad, axis=2, keepdims=True)
        score_grad = (attn_prob * (prob_grad - row_inner)).astype(jnp.bfloat16)
        key_parts.append(
            jnp.einsum("hqk,qhd->kd", score_grad, q_block, preferred_element_type=jnp.float32)
            * score_scale
        )
        query_part = (
            jnp.einsum("hqk,kd->qhd", score_grad, k_block, preferred_element_type=jnp.float32)
            * score_scale
        )
        query_parts.append(query_part.reshape(tok_rows, group_size * HD).astype(jnp.bfloat16))
    return (
        jnp.concatenate(query_parts, axis=1),
        jnp.concatenate(key_parts, axis=1),
        jnp.concatenate(value_parts, axis=1),
    )


def shards(hidden, norm_gain, kv_weight, queries, out_grad):
    half_cols = kv_weight.shape[1] // 2
    hidden_f = hidden.astype(jnp.float32)
    squares = lax.psum(jnp.sum(hidden_f * hidden_f, axis=1), "section")
    inv_rms = lax.rsqrt(squares / D + EPSILON)
    normed = (hidden_f * inv_rms[:, None] * norm_gain[None, :]).astype(jnp.bfloat16)
    kv_local = jnp.dot(normed, kv_weight, preferred_element_type=jnp.float32)
    kv_all = lax.psum(kv_local, "section").astype(jnp.bfloat16)
    key_rows = kv_all[:, :half_cols]
    value_rows = kv_all[:, half_cols:]
    query_grad, key_part, value_part = attend(queries, key_rows, value_rows, out_grad)
    local_grad = jnp.concatenate([key_part, value_part], axis=1)
    kv_grad = lax.psum(local_grad, "section").astype(jnp.bfloat16)
    weight_term = lax.dot_general(
        normed, kv_grad, (((0,), (0,)), ((), ())), preferred_element_type=jnp.float32
    )
    normed_full = lax.dot_general(
        kv_grad, kv_weight, (((1,), (1,)), ((), ())), preferred_element_type=jnp.float32
    )
    gain_term = jnp.sum(normed_full * hidden_f * inv_rms[:, None], axis=0)
    weight_sum, gain_sum = lax.psum((weight_term, gain_term), "dp")
    replicas = lax.axis_size("dp")
    return (
        query_grad,
        weight_sum / replicas,
        gain_sum / replicas,
        normed_full.astype(jnp.bfloat16),
    )


def solution(mesh):
    placed = (
        P("dp", "section"),
        P("section"),
        P("section", None),
        P("dp", "section"),
        P("dp", "section"),
    )
    return jax.shard_map(
        shards,
        mesh=mesh,
        in_specs=placed,
        out_specs=(P("dp", "section"), P("section", None), P("section"), P("dp", "section")),
        check_vma=False,
    )
```

profile of v0, /device:TPU:1, one launch (start us, length us, event | category | flops | bytes accessed | tf_op | source)
XLA Modules:
  0.0 443.9 jit_solution(14795855018364282509)
XLA Ops:
  8.4 17.2 %psum.35 = f32[192]{0:T(256)S(1)} all-reduce(f32[192]{0:T(256)S(1)} %fusion.40), channel_id=1, replica_groups=mesh['dp'=32,'section'=8] {'section'}, use_global_device_ids=true, to_apply=%region_1.0 | all-reduce | flops 192 | bytes 1536 | tf_op jit(solution)/shard_map/psum | solution.py:66
  25.6 1.5 fusion.54
  27.1 38.4 %all-reduce.5 = bf16[192,1024]{1,0:T(8,128)(2,1)} all-reduce(f32[192,1024]{1,0:T(8,128)S(1)} %fusion.54), channel_id=1, replica_groups=mesh['dp'=32,'section'=8] {'section'}, use_global_device_ids=true, to_apply=%region_2.0 | all-reduce | flops 196608 | bytes 1179648 | tf_op jit(solution)/shard_map/psum | solution.py:70
  65.5 1.4 fusion.68
  67.7 2.2 fusion.69
  69.9 1.8 copy.15
  74.5 2.2 fusion.72
  76.6 2.2 fusion.71
  78.9 1.4 fusion.73
  80.3 1.4 fusion.74
  81.7 1.6 multiply_reduce_fusion.3
  91.0 2.4 fusion.31
  93.3 2.4 fusion.30
  95.7 2.4 fusion.29
  98.1 2.4 fusion.28
  100.5 41.0 %all-reduce.6 = bf16[192,1024]{1,0:T(8,128)(2,1)} all-reduce(f32[192,1024]{1,0:T(8,128)} %fusion.28), channel_id=1, replica_groups=mesh['dp'=32,'section'=8] {'section'}, use_global_device_ids=true, to_apply=%region_15.16 | all-reduce | flops 196608 | bytes 1179648 | tf_op jit(solution)/shard_map/psum | solution.py:75
  141.5 3.1 fusion.51
  144.7 1.9 fusion.25
  146.5 1.8 copy.30
  154.6 1.5 pad_maximum_fusion
  156.1 1.4 copy.45
  158.8 81.6 %psum.39 = f32[640]{0:T(1024)S(1)} all-reduce(f32[640]{0:T(1024)S(1)} %get-tuple-element.17), channel_id=1, replica_groups=mesh['dp'=32,'section'=8] {'dp'}, use_global_device_ids=true, to_apply=%region_18.19 | all-reduce | flops 640 | bytes 5120 | tf_op jit(solution)/shard_map/psum | solution.py:83
  240.9 192.5 %all-reduce.4.cloned.1.call-done = f32[640,1024]{1,0:T(8,128)} async-done(((f32[640,1024]{1,0:T(8,128)}), f32[640,1024]{1,0:T(8,128)}) %all-reduce.4.cloned.1.call-update) | async-done | bytes 2621456 | tf_op jit(solution)/shard_map/psum | solution.py:83
  433.4 3.7 broadcast_multiply_fusion
  (73 shorter events, 20.4 us)
Async XLA Ops:
  7.2 18.5 %copy-start = (bf16[640,1024]{1,0:T(8,128)(2,1)S(1)}, bf16[640,1024]{1,0:T(8,128)(2,1)}, u32[]{:S(2)}) copy-start(bf16[640,1024]{1,0:T(8,128)(2,1)} %param.7) | copy-start | bytes 3932164
  7.2 426.2 %all-reduce.4.cloned.1.call-start = ((), (), s32[]{:S(2)}) async-start(), calls=%async_computation | async-start | bytes 5242880 | tf_op jit(solution)/shard_map/psum | solution.py:83
  7.3 88.4 %copy-start.19 = (pred[192,192]{0,1:T(8,128)(4,1)}, pred[192,192]{0,1:T(8,128)(4,1)S(1)}, u32[]{:S(2)}) copy-start(pred[192,192]{0,1:T(8,128)(4,1)S(1)} %iota_compare_fusion) | copy-start | bytes 110596
  67.1 16.4 %copy-start.9 = (bf16[192,640]{0,1:T(8,128)(2,1)}, bf16[192,640]{0,1:T(8,128)(2,1)S(1)}, u32[]{:S(2)}) copy-start(bf16[192,640]{0,1:T(8,128)(2,1)S(1)} %copy.13) | copy-start | bytes 737284
  67.3 16.0 %copy-start.5 = (bf16[192,640]{0,1:T(8,128)(2,1)}, bf16[192,640]{0,1:T(8,128)(2,1)S(1)}, u32[]{:S(2)}) copy-start(bf16[192,640]{0,1:T(8,128)(2,1)S(1)} %copy.19) | copy-start | bytes 737284
  67.5 15.8 %copy-start.3 = (bf16[192,640]{0,1:T(8,128)(2,1)}, bf16[192,640]{0,1:T(8,128)(2,1)S(1)}, u32[]{:S(2)}) copy-start(bf16[192,640]{0,1:T(8,128)(2,1)S(1)} %copy.31) | copy-start | bytes 737284
  67.7 9.0 %copy-start.7 = (bf16[192,640]{0,1:T(8,128)(2,1)}, bf16[192,640]{0,1:T(8,128)(2,1)S(1)}, u32[]{:S(2)}) copy-start(bf16[192,640]{0,1:T(8,128)(2,1)S(1)} %copy.25) | copy-start | bytes 737284
  73.5 5.3 %copy-start.14 = (bf16[192,1024]{1,0:T(8,128)(2,1)S(1)}, bf16[192,1024]{1,0:T(8,128)(2,1)}, u32[]{:S(2)}) copy-start(bf16[192,1024]{1,0:T(8,128)(2,1)} %all-reduce.5) | copy-start | bytes 1179652
  76.6 5.1 %copy-start.18 = (bf16[192,640]{0,1:T(8,128)(2,1)S(1)}, bf16[192,640]{0,1:T(8,128)(2,1)}, u32[]{:S(2)}) copy-start(bf16[192,640]{0,1:T(8,128)(2,1)} %copy.15) | copy-start | bytes 737284
  81.7 1.6 copy-start.13
  83.3 1.2 copy-start.12
  83.3 1.3 copy-start.17
  84.6 1.2 copy-start.11
  84.6 1.3 copy-start.15
  85.9 1.2 copy-start.10
  85.9 1.3 copy-start.16
  87.1 1.0 copy-start.6
  87.4 1.6 copy-start.8
  87.4 2.6 copy-start.4
  98.1 43.5 %copy-start.1 = (bf16[192,640]{1,0:T(8,128)(2,1)S(1)}, bf16[192,640]{1,0:T(8,128)(2,1)}, u32[]{:S(2)}) copy-start(bf16[192,640]{1,0:T(8,128)(2,1)} %param.5) | copy-start | bytes 737284
  98.1 43.5 %copy-start.20 = (f32[640]{0:T(1024)S(1)}, f32[640]{0:T(1024)}, u32[]{:S(2)}) copy-start(f32[640]{0:T(1024)} %param.6) | copy-start | bytes 7684
  153.7 3.8 copy-start.2
Sparse Core Ops, SparseCore 0:
  144.8 288.5 all-reduce.3
where the time goes:
time: 445 us; the launch traced here: 444 us
  waiting for transfers between devices  192 us (43%)
  blocking collectives  178 us (40%)
  matrix products  34.3 us (8%)
  local copies, waits for them, and re-layouts  17.1 us (4%)
  between operations  14.3 us (3%)
  other arithmetic  7.55 us (2%)
    psum x1, waiting for transfers between devices, shards(): weight_sum, gain_sum = lax.psum((weight_term, gain_term), 'dp')  192 us
    psum x1, blocking collectives, shards(): weight_sum, gain_sum = lax.psum((weight_term, gain_term), 'dp')  81.6 us
    psum x1, blocking collectives, shards(): kv_grad = lax.psum(local_grad, 'section').astype(jnp.bfloat16)  41 us
    psum x1, blocking collectives, shards(): kv_all = lax.psum(kv_local, 'section').astype(jnp.bfloat16)  38.4 us
    psum x1, blocking collectives, shards(): squares = lax.psum(jnp.sum(hidden_f * hidden_f, axis=1), 'section')  17.2 us
    dot_general x4, matrix products, attend(): jnp.einsum('hqk,qhd->kd', prob_low, g_block, preferred_element_type=jnp.f...  9.52 us
  transfers between devices with their start and end apart: 1, of which 1 were waited for; matrix products, arithmetic and copies ran while one was open for 3% of the time, Pallas kernels for 0%

commit v1 on v0

v1 whole, which is shorter than its diff:
```python
import jax
import jax.numpy as jnp
from jax import lax
from jax.experimental import pallas as pl
from jax.experimental.pallas import tpu as pltpu
from jax.sharding import PartitionSpec as P

D = 5120
HD = 128
KVH = 4
QH = 20
GRP = QH // KVH
NSEC = 8
NZ = 8
TOK = 192
FEAT = 640
HALF = FEAT // 2
RB = 48
EPSILON = 1e-05
SCALE = HD ** (-0.5)
MESH = pl.DeviceIdType.MESH
F32 = jnp.float32
BF16 = jnp.bfloat16

NT = (((1,), (1,)), ((), ()))
NN = (((1,), (0,)), ((), ()))
TN = (((0,), (0,)), ((), ()))


def dot(a, b, dims=NN):
    return lax.dot_general(a, b, dims, preferred_element_type=F32)


def fused_kernel(
    h_hbm, gain_hbm, w_hbm, q_hbm, g_hbm,
    qg_out, wg_out, gg_out, ng_out,
    h_v, gain_v, w_v, q_v, g_v, qg_v, ng_v,
    ss, nrm, nT, nTp,
    part_a, rs_a, kvb, part_b, rs_b, kvg, kvgp,
    pbuf_a, dsbuf_a, pbuf_b, dsbuf_b, nf,
    wp, rz, xs, xr, wgb, gpair, gz, gx,
    loc, out_sem,
    ss_s, ss_r, nt_s, nt_r,
    ra_s, ra_r, aa_s, aa_r, rb_s, rb_r, ab_s, ab_r,
    kp_s, kp_r, rz_s, rz_r, x_s, x_r, az_s, az_r, cc_s, cc_r,
    gp_s, gp_r, gz_s, gz_r, gx_s, gx_r,
):
    dp = lax.axis_index("dp")
    sec = lax.axis_index("section")
    core = lax.rem(dp, 2)
    zz = lax.rem(lax.div(dp, 2), NZ)
    xh = lax.div(dp, 2 * NZ)
    yy = lax.div(sec, 2)
    xl = lax.rem(sec, 2)

    def dp_of(x_, z_, c_):
        return x_ * (2 * NZ) + z_ * 2 + c_

    sec_peer = [None] + [lax.rem(sec + o, NSEC) for o in range(1, NSEC)]
    z_at = [lax.rem(zz + o, NZ) for o in range(NZ)]
    sec_dev = [None] + [(dp, sec_peer[o]) for o in range(1, NSEC)]
    z_dev = [None] + [(dp_of(xh, z_at[o], core), sec) for o in range(1, NZ)]
    core_dev = (dp_of(xh, zz, 1 - core), sec)
    x_dev = (dp_of(1 - xh, zz, core), sec)

    def rcopy(src, dst, s, r, dev):
        return pltpu.make_async_remote_copy(
            src_ref=src, dst_ref=dst, send_sem=s, recv_sem=r, device_id=dev, device_id_type=MESH
        )

    pend = []

    loads = [
        pltpu.make_async_copy(src, dst, loc.at[i])
        for i, (src, dst) in enumerate(
            [(h_hbm, h_v), (gain_hbm, gain_v), (w_hbm, w_v), (q_hbm, q_v), (g_hbm, g_v)]
        )
    ]
    for c in loads:
        c.start()
    bar = pltpu.get_barrier_semaphore()
    partners = sec_dev[1:] + z_dev[1:] + [core_dev, x_dev]
    for dev in partners:
        pl.semaphore_signal(bar, inc=1, device_id=dev, device_id_type=MESH)

    loads[0].wait()
    acc = None
    for t in range(5):
        ht = h_v[:, t * 128:(t + 1) * 128].astype(F32)
        acc = ht * ht if acc is None else acc + ht * ht
    row = jnp.sum(acc.T, axis=0, keepdims=True)
    ss[0] = jnp.broadcast_to(row, (8, TOK))
    pl.semaphore_wait(bar, len(partners))
    ss_c = [
        rcopy(ss.at[0], ss.at[o], ss_s.at[o - 1], ss_r.at[o - 1], sec_dev[o]) for o in range(1, NSEC)
    ]
    for c in ss_c:
        c.start()
    loads[1].wait()
    loads[2].wait()
    for c in ss_c:
        c.wait()
    tot = ss[0]
    for o in range(1, NSEC):
        tot = tot + ss[o]
    inv_row = lax.rsqrt(tot[0:1, :] / D + EPSILON)
    inv = jnp.broadcast_to(inv_row, (128, TOK)).T
    for t in range(5):
        cols = slice(t * 128, (t + 1) * 128)
        n_t = (h_v[:, cols].astype(F32) * inv * gain_v[:, cols]).astype(BF16)
        nrm[:, cols] = n_t
        nT[cols, :] = n_t.T

    ra_c = {}
    for j in range(KVH):
        wj = jnp.concatenate(
            [w_v[:, j * 128:(j + 1) * 128], w_v[:, 512 + j * 128:512 + (j + 1) * 128]], axis=1
        )
        pj = dot(nrm[...], wj)
        part_a[j, 0] = pj[:, 0:128]
        part_a[j, 1] = pj[:, 128:256]
        for o in range(1, NSEC):
            d = sec_peer[o]
            c = rcopy(
                part_a.at[j, lax.rem(d, 2), pl.ds(pl.multiple_of(lax.div(d, 2) * RB, RB), RB), :],
                rs_a.at[j, o - 1], ra_s.at[j, o - 1], ra_r.at[j, o - 1], sec_dev[o],
            )
            c.start()
            ra_c[j, o] = c
    other = pl.multiple_of((1 - core) * HALF, 16)
    nt_c = rcopy(nT.at[pl.ds(other, HALF), :], nTp, nt_s.at[0], nt_r.at[0], core_dev)
    nt_c.start()
    loads[3].wait()
    loads[4].wait()
    my_rows = pl.ds(pl.multiple_of(yy * RB, RB), RB)

    ag = {}

    def reduce_and_gather(j, copies, part, rs, dst, s, r, tag):
        tot = part[j, xl, my_rows, :]
        for o in range(1, NSEC):
            copies[j, o].wait()
        for o in range(1, NSEC):
            tot = tot + rs[j, o - 1]
        dst[j, xl, my_rows, :] = tot.astype(BF16)
        for o in range(1, NSEC):
            piece = dst.at[j, xl, my_rows, :]
            c = rcopy(piece, piece, s.at[j, o - 1], r.at[j, o - 1], sec_dev[o])
            c.start()
            ag[tag, j, o] = c

    def wait_gather(j, tag):
        for o in range(1, NSEC):
            ag[tag, j, o].wait()

    def do_r(j):
        reduce_and_gather(j, ra_c, part_a, rs_a, kvb, aa_s, aa_r, "a")

    mask_a = (
        lax.broadcasted_iota(jnp.int32, (128, 128), 0)
        <= lax.broadcasted_iota(jnp.int32, (128, 128), 1)
    )
    qpos = lax.broadcasted_iota(jnp.int32, (64, 128), 1)
    mask_b = lax.broadcasted_iota(jnp.int32, (64, 128), 0) <= jnp.where(qpos < 64, qpos, qpos - 64)
    rb_c = {}
    qg_c = {}

    def soft(s, dpr):
        m = jnp.max(s, axis=0, keepdims=True)
        e = jnp.exp(s - m)
        p = e * (1.0 / jnp.sum(e, axis=0, keepdims=True))
        inner = jnp.sum(p * dpr, axis=0, keepdims=True)
        return p.astype(BF16), (p * (dpr - inner)).astype(BF16)

    def do_t(j):
        wait_gather(j, "a")
        k = kvb[j, 0]
        v = kvb[j, 1]
        k_lo = k[0:128]
        v_lo = v[0:128]
        col0 = j * GRP * HD

        def heads(ref, rows, hs):
            return [ref[rows, col0 + h * HD:col0 + (h + 1) * HD] for h in hs]

        lo, hi = slice(0, 128), slice(128, TOK)
        for h in range(GRP):
            qh = heads(q_v, lo, [h])[0]
            gh = heads(g_v, lo, [h])[0]
            s = jnp.where(mask_a, dot(k_lo, qh, NT) * SCALE, -1e30)
            p, ds = soft(s, dot(v_lo, gh, NT))
            pbuf_a[:, h * 128:(h + 1) * 128] = p
            dsbuf_a[:, h * 128:(h + 1) * 128] = ds
        q_hi = jnp.concatenate(heads(q_v, hi, range(GRP)) + heads(q_v, hi, [GRP - 1]), axis=0)
        g_hi = jnp.concatenate(heads(g_v, hi, range(GRP)) + heads(g_v, hi, [GRP - 1]), axis=0)
        for i in range(3):
            qh = q_hi[i * 128:(i + 1) * 128]
            gh = g_hi[i * 128:(i + 1) * 128]
            s = dot(k, qh, NT) * SCALE
            s = jnp.concatenate([s[0:128], jnp.where(mask_b, s[128:TOK], -1e30)], axis=0)
            p, ds = soft(s, dot(v, gh, NT))
            pbuf_b[:, i * 128:(i + 1) * 128] = p
            dsbuf_b[:, i * 128:(i + 1) * 128] = ds
        q_lo = jnp.concatenate(heads(q_v, lo, range(GRP)), axis=0)
        g_lo = jnp.concatenate(heads(g_v, lo, range(GRP)), axis=0)
        nb = 64 * GRP
        kb = dot(dsbuf_b[:, 0:nb], q_hi[0:nb])
        vb = dot(pbuf_b[:, 0:nb], g_hi[0:nb])
        ka = dot(dsbuf_a[...], q_lo)
        va = dot(pbuf_a[...], g_lo)
        part_b[j, 0, 0:128] = (ka + kb[0:128]) * SCALE
        part_b[j, 0, 128:TOK] = kb[128:TOK] * SCALE
        part_b[j, 1, 0:128] = va + vb[0:128]
        part_b[j, 1, 128:TOK] = vb[128:TOK]
        for o in range(1, NSEC):
            d = sec_peer[o]
            c = rcopy(
                part_b.at[j, lax.rem(d, 2), pl.ds(pl.multiple_of(lax.div(d, 2) * RB, RB), RB), :],
                rs_b.at[j, o - 1], rb_s.at[j, o - 1], rb_r.at[j, o - 1], sec_dev[o],
            )
            c.start()
            rb_c[j, o] = c
        qa = dot(dsbuf_a[...], k_lo, TN) * SCALE
        qb = dot(dsbuf_b[:, 0:nb], k, TN) * SCALE
        for h in range(GRP):
            qg_v[0:128, col0 + h * HD:col0 + (h + 1) * HD] = qa[h * 128:(h + 1) * 128].astype(BF16)
            qg_v[128:TOK, col0 + h * HD:col0 + (h + 1) * HD] = qb[h * 64:(h + 1) * 64].astype(BF16)
        c = pltpu.make_async_copy(
            qg_v.at[:, col0:col0 + GRP * HD], qg_out.at[:, col0:col0 + GRP * HD], out_sem.at[j]
        )
        c.start()
        qg_c[j] = c

    def do_u(j):
        reduce_and_gather(j, rb_c, part_b, rs_b, kvg, ab_s, ab_r, "b")

    kp_c = {}

    def do_x(j):
        wait_gather(j, "b")
        c = rcopy(kvg.at[j], kvgp.at[j], kp_s.at[j], kp_r.at[j], core_dev)
        c.start()
        kp_c[j] = c

    def ring(j, d):
        sign = 1 if d == 0 else -1
        hops = 4 if (j + d) % 2 == 0 else 3
        slot0 = 0 if d == 0 else 4
        return sign, hops, slot0

    rz_c = {}

    def send_ring(j, d, s):
        sign, hops, slot0 = ring(j, d)
        chunk = z_at[(sign * (hops - s)) % NZ]
        if s == 0:
            src = wp.at[j, chunk]
        else:
            rz_c[j, d, s - 1].wait()
            rz[j, slot0 + s - 1] = rz[j, slot0 + s - 1] + wp[j, chunk]
            src = rz.at[j, slot0 + s - 1]
        c = rcopy(
            src, rz.at[j, slot0 + s], rz_s.at[j, slot0 + s], rz_r.at[j, slot0 + s], z_dev[sign % NZ]
        )
        c.start()
        rz_c[j, d, s] = c

    def do_y(j):
        if j == 0:
            nt_c.wait()
        kp_c[j].wait()
        mine = pl.ds(pl.multiple_of(core * HALF, 16), HALF)
        both = jnp.concatenate([kvg[j, 0], kvg[j, 1]], axis=1)
        both_p = jnp.concatenate([kvgp[j, 0], kvgp[j, 1]], axis=1)
        prod = dot(nT[mine, :], both) + dot(nTp[...], both_p)
        for r in range(4):
            for cb in range(2):
                wp[j, 2 * r + cb] = prod[r * 80:(r + 1) * 80, cb * 128:(cb + 1) * 128]
        send_ring(j, 0, 0)
        send_ring(j, 1, 0)

    def do_nf(j):
        both = jnp.concatenate([kvg[j, 0], kvg[j, 1]], axis=1)
        wj = jnp.concatenate(
            [w_v[:, j * 128:(j + 1) * 128], w_v[:, 512 + j * 128:512 + (j + 1) * 128]], axis=1
        )
        term = dot(both, wj, NT)
        nf[...] = term if j == 0 else nf[...] + term

    g_c = {}

    def do_gain():
        gpair[0] = jnp.zeros((8, 128), F32)
        for t in range(5):
            cols = slice(t * 128, (t + 1) * 128)
            full = nf[:, cols]
            ng_v[:, cols] = full.astype(BF16)
            term = full * h_v[:, cols].astype(F32) * inv
            gpair[0, t:t + 1, :] = jnp.sum(term, axis=0, keepdims=True)
        c = rcopy(gpair.at[0], gpair.at[1], gp_s.at[0], gp_r.at[0], core_dev)
        c.start()
        g_c["p"] = c
        c = pltpu.make_async_copy(ng_v, ng_out, out_sem.at[4])
        c.start()
        g_c["ng"] = c

    def do_gain_z():
        g_c["p"].wait()
        gz[zz] = gpair[0] + gpair[1]
        for o in range(1, NZ):
            c = rcopy(gz.at[zz], gz.at[zz], gz_s.at[o - 1], gz_r.at[o - 1], z_dev[o])
            c.start()
            g_c[o] = c

    def do_gain_x():
        for o in range(1, NZ):
            g_c[o].wait()
        tot = gz[0]
        for i in range(1, NZ):
            tot = tot + gz[i]
        gx[0] = tot
        c = rcopy(gx.at[0], gx.at[1], gx_s.at[0], gx_r.at[0], x_dev)
        c.start()
        g_c["x"] = c

    def do_gain_end():
        g_c["x"].wait()
        gx[2] = (gx[0] + gx[1]) * (1.0 / 32.0)
        c = pltpu.make_async_copy(gx.at[2], gg_out, out_sem.at[5])
        c.start()
        g_c["out"] = c

    def do_z(j, s):
        for d in range(2):
            if s < ring(j, d)[1]:
                send_ring(j, d, s)

    x_c = {}

    def do_xx(j):
        tot = wp[j, zz]
        for d in range(2):
            _, hops, slot0 = ring(j, d)
            rz_c[j, d, hops - 1].wait()
            tot = tot + rz[j, slot0 + hops - 1]
        xs[j] = tot
        c = rcopy(xs.at[j], xr.at[j], x_s.at[j], x_r.at[j], x_dev)
        c.start()
        x_c[j] = c

    az_c = {}

    def fwd(j, d, s):
        sign, hops, slot0 = ring(j, d)
        if s > 0:
            az_c[j, d, s - 1].wait()
        if s < hops:
            chunk = z_at[(-sign * s) % NZ]
            piece = wgb.at[core, j, chunk]
            c = rcopy(piece, piece, az_s.at[j, slot0 + s], az_r.at[j, slot0 + s], z_dev[sign % NZ])
            c.start()
            az_c[j, d, s] = c

    def do_g(j, s):
        if s == 0:
            x_c[j].wait()
            wgb[core, j, zz] = ((xs[j] + xr[j]) * (1.0 / 32.0)).astype(BF16)
        for d in range(2):
            if s <= ring(j, d)[1]:
                fwd(j, d, s)

    cc_c = {}

    def do_cc(j):
        piece = wgb.at[core, j]
        c = rcopy(piece, piece, cc_s.at[j], cc_r.at[j], core_dev)
        c.start()
        cc_c[j] = c

    wo_c = {}

    def do_out(j):
        cc_c[j].wait()
        for half in range(2):
            c = pltpu.make_async_copy(wgb.at[half, j], wg_out.at[half, j], out_sem.at[6 + 2 * j + half])
            c.start()
            wo_c[j, half] = c

    tasks = []
    for j in range(KVH):
        tasks.append((5.4 + 2.1 * j, do_r, (j,)))
        tasks.append((9.7 + 2.1 * j, do_t, (j,)))
        b0 = 17.0 + 3.0 * j
        tasks.append((b0, do_u, (j,)))
        tasks.append((b0 + 4.4, do_x, (j,)))
        tasks.append((b0 + 5.7, do_y, (j,)))
        tasks.append((b0 + 5.8, do_nf, (j,)))
        for s in range(1, 4):
            tasks.append((b0 + 5.7 + 2.6 * s, do_z, (j, s)))
        tasks.append((b0 + 16.1, do_xx, (j,)))
        for s in range(0, 5):
            tasks.append((b0 + 18.6 + 2.2 * s, do_g, (j, s)))
        tasks.append((b0 + 27.5, do_cc, (j,)))
        tasks.append((b0 + 28.8, do_out, (j,)))
    last = 17.0 + 3.0 * 3
    tasks.append((last + 5.9, do_gain, ()))
    tasks.append((last + 8.4, do_gain_z, ()))
    tasks.append((last + 13.5, do_gain_x, ()))
    tasks.append((last + 18.5, do_gain_end, ()))
    tasks.sort(key=lambda t: t[0])
    for _, f, a in tasks:
        f(*a)

    for j in range(KVH):
        qg_c[j].wait()
        for half in range(2):
            wo_c[j, half].wait()
    g_c["ng"].wait()
    g_c["out"].wait()


def finish_kernel(wgb_ref, out_ref):
    for r in range(4):
        for cb in range(2):
            out_ref[r * 80:(r + 1) * 80, cb * 512:(cb + 1) * 512] = jnp.concatenate(
                [wgb_ref[0, j, 2 * r + cb].astype(F32) for j in range(KVH)], axis=1
            )


def shards(hidden, norm_gain, kv_weight, queries, out_grad):
    any_spec = pl.BlockSpec(memory_space=pl.ANY)
    dma = pltpu.SemaphoreType.DMA
    vm = pltpu.VMEM
    scratch = [
        vm((TOK, FEAT), BF16), vm((1, FEAT), F32), vm((FEAT, 1024), BF16),
        vm((TOK, QH * HD), BF16), vm((TOK, QH * HD), BF16), vm((TOK, QH * HD), BF16), vm((TOK, FEAT), BF16),
        vm((NSEC, 8, TOK), F32), vm((TOK, FEAT), BF16), vm((FEAT, TOK), BF16), vm((HALF, TOK), BF16),
        vm((KVH, 2, TOK, HD), F32), vm((KVH, 7, RB, HD), F32), vm((KVH, 2, TOK, HD), BF16),
        vm((KVH, 2, TOK, HD), F32), vm((KVH, 7, RB, HD), F32), vm((KVH, 2, TOK, HD), BF16),
        vm((KVH, 2, TOK, HD), BF16),
        vm((128, 640), BF16), vm((128, 640), BF16), vm((TOK, 384), BF16), vm((TOK, 384), BF16),
        vm((TOK, FEAT), F32),
        vm((KVH, NZ, 80, 128), F32), vm((KVH, 8, 80, 128), F32), vm((KVH, 80, 128), F32),
        vm((KVH, 80, 128), F32), vm((2, KVH, NZ, 80, 128), BF16),
        vm((2, 8, 128), F32), vm((NZ, 8, 128), F32), vm((3, 8, 128), F32),
        dma((5,)), dma((14,)),
        dma((7,)), dma((7,)), dma((1,)), dma((1,)),
        dma((KVH, 7)), dma((KVH, 7)), dma((KVH, 7)), dma((KVH, 7)),
        dma((KVH, 7)), dma((KVH, 7)), dma((KVH, 7)), dma((KVH, 7)),
        dma((KVH,)), dma((KVH,)), dma((KVH, 8)), dma((KVH, 8)), dma((KVH,)), dma((KVH,)),
        dma((KVH, 8)), dma((KVH, 8)), dma((KVH,)), dma((KVH,)),
        dma((1,)), dma((1,)), dma((7,)), dma((7,)), dma((1,)), dma((1,)),
    ]
    query_grad, wgb, gain8, normed_grad = pl.pallas_call(
        fused_kernel,
        out_shape=(
            jax.ShapeDtypeStruct((TOK, QH * HD), BF16),
            jax.ShapeDtypeStruct((2, KVH, NZ, 80, 128), BF16),
            jax.ShapeDtypeStruct((8, 128), F32),
            jax.ShapeDtypeStruct((TOK, FEAT), BF16),
        ),
        in_specs=[any_spec] * 5,
        out_specs=(any_spec,) * 4,
        scratch_shapes=scratch,
        compiler_params=pltpu.CompilerParams(
            collective_id=0, has_side_effects=True, vmem_limit_bytes=40 * 1024 * 1024
        ),
        name="fused",
    )(hidden, norm_gain.reshape(1, FEAT), kv_weight, queries, out_grad)
    weight_grad = pl.pallas_call(
        finish_kernel,
        grid=(2,),
        out_shape=jax.ShapeDtypeStruct((FEAT, 1024), F32),
        in_specs=[pl.BlockSpec((1, KVH, NZ, 80, 128), lambda i: (i, 0, 0, 0, 0))],
        out_specs=pl.BlockSpec((HALF, 1024), lambda i: (i, 0)),
        name="finish",
    )(wgb)
    return query_grad, weight_grad, gain8[:5].reshape(FEAT), normed_grad


def solution(mesh):
    placed = (
        P("dp", "section"),
        P("section"),
        P("section", None),
        P("dp", "section"),
        P("dp", "section"),
    )
    return jax.shard_map(
        shards,
        mesh=mesh,
        in_specs=placed,
        out_specs=(P("dp", "section"), P("section", None), P("section"), P("dp", "section")),
        check_vma=False,
    )
```

time: 445 us -> 102 us (0.23)
  waiting for transfers between devices: 192 us -> 0 us
  blocking collectives: 178 us -> 0 us
  Pallas kernels: 0 us -> 92.8 us
  matrix products: 34.3 us -> 0 us
  between operations: 14.3 us -> 0.65 us
  local copies, waits for them, and re-layouts: 17.1 us -> 8.64 us
  other arithmetic: 7.55 us -> 0 us
    psum x1 -> x0, waiting for transfers between devices: 192 us -> none  [shards(): weight_sum, gain_sum = lax.psum((weight_term, gain_term), 'dp')]
    psum x4 -> x0, blocking collectives: 178 us -> none  [the longest x1 81.6 us: shards(): weight_sum, gain_sum = lax.psum((weight_term, gain_term), 'dp')]
    pallas_call x0 -> x2, Pallas kernels: none -> 92.8 us  [the longest x1 90.1 us: shards(): pl.pallas_call(fused_kernel, out_shape=(jax.ShapeDtypeStruct((TOK, QH * H...]
    dot_general x19 -> x0, matrix products: 27.1 us -> none  [the longest x4 9.52 us: attend(): jnp.einsum('hqk,qhd->kd', prob_low, g_block, preferred_element_type=jnp.f...]
    slice x10 -> x0, local copies, waits for them, and re-layouts: 8.87 us -> none  [the longest x5 6.75 us: attend(): grad_layer[:, first_col:last_col].reshape(tok_rows, group_size, HD)]
    sub x4 -> x0, matrix products: 7.26 us -> none  [attend(): weights = jnp.exp(scores - row_max)]
    convert_element_type x4 -> x0, local copies, waits for them, and re-layouts: 4.55 us -> none  [attend(): query_part.reshape(tok_rows, group_size * HD).astype(jnp.bfloat16)]
  transfers between devices with their start and end apart: 1 -> 0, of which waited for: 1 -> 0; matrix products, arithmetic and copies ran while one was open for 3% -> 0% of each run, Pallas kernels for 0% -> 0%
where the time goes in v1:
time: 102 us
  Pallas kernels  92.8 us (91%)
  local copies, waits for them, and re-layouts  8.64 us (8%)
    pallas_call x1, Pallas kernels, shards(): pl.pallas_call(fused_kernel, out_shape=(jax.ShapeDtypeStruct((TOK, QH * H...  90.1 us
    unnamed x12, local copies, waits for them, and re-layouts  7.36 us
    pallas_call x1, Pallas kernels, shards(): pl.pallas_call(finish_kernel, grid=(2,), out_shape=jax.ShapeDtypeStruct((...  2.66 us

profile of v1, /device:TPU:1, one launch (start us, length us, event | category | flops | bytes accessed | tf_op | source)
XLA Modules:
  0.0 102.1 jit_solution(17057604110628832824)
XLA Ops:
  0.6 0.7 reshape.14.gain_hbm
  1.3 0.0 copy-start
  1.3 1.3 %copy-done = bf16[640,1024]{1,0:T(8,128)(2,1)S(1)} copy-done((bf16[640,1024]{1,0:T(8,128)(2,1)S(1)}, bf16[640,1024]{1,0:T(8,128)(2,1)}, u32[]{:S(2)}) %copy-start) | copy-done | bytes 1310744
  2.6 0.0 copy-start.2
  2.6 1.2 %copy-done.2 = bf16[192,2560]{1,0:T(8,128)(2,1)S(1)} copy-done((bf16[192,2560]{1,0:T(8,128)(2,1)S(1)}, bf16[192,2560]{1,0:T(8,128)(2,1)}, u32[]{:S(2)}) %copy-start.2) | copy-done | bytes 983064
  3.8 0.0 copy-start.3
  3.8 1.2 %copy-done.3 = bf16[192,2560]{1,0:T(8,128)(2,1)S(1)} copy-done((bf16[192,2560]{1,0:T(8,128)(2,1)S(1)}, bf16[192,2560]{1,0:T(8,128)(2,1)}, u32[]{:S(2)}) %copy-start.3) | copy-done | bytes 983064
  5.0 0.0 copy-start.4
  5.0 0.9 copy-done.4
  6.0 90.1 %fused.1 = (bf16[192,2560]{1,0:T(8,128)(2,1)S(1)}, bf16[2,4,8,80,128]{4,3,2,1,0:T(8,128)(2,1)S(1)}, f32[8,128]{1,0:T(8,128)S(1)}, bf16[192,640]{1,0:T(8,128)(2,1)S(1)}) custom-call(bf16[192,640]{1,0:T(8,128)(2,1)S(1)} %copy-done.4, f32[1,640]{1,0:T(1,128)S(1)} %reshape.14.gain_hbm, bf16[640,1024]{1,0:T(8,128)(2,1)S(1)} %copy-done, ...), custom_call_target="tpu_custom_call" | custom-call | tf_op jit(solution)/shard_map/fused/pallas_call | solution.py:454
  96.1 0.0 copy-start.1
  96.1 1.1 %copy-done.1 = bf16[2,4,8,80,128]{4,3,2,1,0:T(8,128)(2,1)} copy-done((bf16[2,4,8,80,128]{4,3,2,1,0:T(8,128)(2,1)}, bf16[2,4,8,80,128]{4,3,2,1,0:T(8,128)(2,1)S(1)}, u32[]{:S(2)}) %copy-start.1) | copy-done | bytes 1310744
  97.2 0.6 slice_bitcast_fusion
  97.8 2.7 %finish.1 = f32[640,1024]{1,0:T(8,128)} custom-call(bf16[2,4,8,80,128]{4,3,2,1,0:T(8,128)(2,1)} %copy-done.1), custom_call_target="tpu_custom_call" | custom-call | tf_op jit(solution)/shard_map/finish/pallas_call | solution.py:470
  100.5 0.9 copy.11
  101.4 0.7 copy.12
Async XLA Ops:
  1.3 1.3 %copy-start = (bf16[640,1024]{1,0:T(8,128)(2,1)S(1)}, bf16[640,1024]{1,0:T(8,128)(2,1)}, u32[]{:S(2)}) copy-start(bf16[640,1024]{1,0:T(8,128)(2,1)} %w_hbm.1) | copy-start | bytes 3932164
  2.6 1.2 %copy-start.2 = (bf16[192,2560]{1,0:T(8,128)(2,1)S(1)}, bf16[192,2560]{1,0:T(8,128)(2,1)}, u32[]{:S(2)}) copy-start(bf16[192,2560]{1,0:T(8,128)(2,1)} %q_hbm.1) | copy-start | bytes 2949124
  3.8 1.2 %copy-start.3 = (bf16[192,2560]{1,0:T(8,128)(2,1)S(1)}, bf16[192,2560]{1,0:T(8,128)(2,1)}, u32[]{:S(2)}) copy-start(bf16[192,2560]{1,0:T(8,128)(2,1)} %g_hbm.1) | copy-start | bytes 2949124
  5.0 0.9 copy-start.4
  96.1 1.1 %copy-start.1 = (bf16[2,4,8,80,128]{4,3,2,1,0:T(8,128)(2,1)}, bf16[2,4,8,80,128]{4,3,2,1,0:T(8,128)(2,1)S(1)}, u32[]{:S(2)}) copy-start(bf16[2,4,8,80,128]{4,3,2,1,0:T(8,128)(2,1)S(1)} %get-tuple-element.9.wgb_ref) | copy-start | bytes 3932164

commit v2 on v1

v2 whole, which is shorter than its diff:
```python
import jax
import jax.numpy as jnp
from jax import lax
from jax.experimental import pallas as pl
from jax.experimental.pallas import tpu as pltpu
from jax.sharding import PartitionSpec as P

D = 5120
HD = 128
KVH = 4
QH = 20
GRP = QH // KVH
NSEC = 8
NZ = 8
TOK = 192
FEAT = 640
HALF = FEAT // 2
RB = 48
AHEAD = 4
DIRECT = (0, 1, 2, 3)
EPSILON = 1e-05
SCALE = HD ** (-0.5)
MESH = pl.DeviceIdType.MESH
F32 = jnp.float32
BF16 = jnp.bfloat16

NT = (((1,), (1,)), ((), ()))
NN = (((1,), (0,)), ((), ()))
TN = (((0,), (0,)), ((), ()))


def dot(a, b, dims=NN):
    return lax.dot_general(a, b, dims, preferred_element_type=F32)


def fused_kernel(
    h_hbm, gain_hbm, w_hbm, q_hbm, g_hbm,
    qg_v, wg_v, gx, ng_v,
    h_v, gain_v, w_v, q_v, g_v,
    ss, ngat,
    part_a, rs_a, st_a, kvb, part_b, rs_b, st_b, kvg, kvt, kvr,
    pbuf_a, dsbuf_a, pbuf_b, dsbuf_b, nf,
    xs, xr, wgb, gpair, gz,
    loc, ss_s, ss_r, ng_s, ng_r, nc_s, nc_r,
    ra_s, ra_r, aa_s, aa_r, rb_s, rb_r, ab_s, ab_r,
    kt_s, ku_s, kt_r, x_s, x_r, az_s, az_r, cc_s, cc_r,
    gp_s, gp_r, gz_s, gz_r, gx_s, gx_r,
):
    dp = lax.axis_index("dp")
    sec = lax.axis_index("section")
    core = lax.rem(dp, 2)
    zz = lax.rem(lax.div(dp, 2), NZ)
    xh = lax.div(dp, 2 * NZ)
    yy = lax.div(sec, 2)
    xl = lax.rem(sec, 2)

    def dp_of(x_, z_, c_):
        return x_ * (2 * NZ) + z_ * 2 + c_

    sec_peer = [None] + [lax.rem(sec + o, NSEC) for o in range(1, NSEC)]
    z_at = [lax.rem(zz + o, NZ) for o in range(NZ)]
    sec_dev = [None] + [(dp, sec_peer[o]) for o in range(1, NSEC)]
    z_dev = [None] + [(dp_of(xh, z_at[o], core), sec) for o in range(1, NZ)]
    z_dev2 = [(dp_of(xh, z_at[o], 1 - core), sec) for o in range(NZ)]
    core_dev = z_dev2[0]
    x_dev = (dp_of(1 - xh, zz, core), sec)

    def rcopy(src, dst, s, r, dev):
        return pltpu.make_async_remote_copy(
            src_ref=src, dst_ref=dst, send_sem=s, recv_sem=r, device_id=dev, device_id_type=MESH
        )

    def wait_bytes(ref, sem):
        pltpu.make_async_copy(ref, ref, sem).wait()

    sends = []

    def start(c):
        c.start()
        sends.append(c.wait_send)

    def send_total(ref, sem):
        sends.append(lambda: wait_bytes(ref, sem))

    loads = [
        pltpu.make_async_copy(src, dst, loc.at[i])
        for i, (src, dst) in enumerate(
            [(h_hbm, h_v), (gain_hbm, gain_v.at[0]), (w_hbm, w_v), (q_hbm, q_v), (g_hbm, g_v)]
        )
    ]
    for c in loads:
        c.start()
    bar = pltpu.get_barrier_semaphore()
    partners = sec_dev[1:] + z_dev[1:] + z_dev2 + [x_dev]
    for dev in partners:
        pl.semaphore_signal(bar, inc=1, device_id=dev, device_id_type=MESH)

    loads[0].wait()
    acc = None
    for t in range(5):
        ht = h_v[:, t * 128:(t + 1) * 128].astype(F32)
        acc = ht * ht if acc is None else acc + ht * ht
    row = jnp.sum(acc.T, axis=0, keepdims=True)
    ss[0] = row
    pl.semaphore_wait(bar, len(partners))
    for o in range(1, NSEC):
        rcopy(ss.at[0], ss.at[o], ss_s.at[0], ss_r.at[0], sec_dev[o]).start()
    send_total(ss.at[1:NSEC], ss_s.at[0])
    loads[1].wait()
    loads[2].wait()
    wait_bytes(ss.at[1:NSEC], ss_r.at[0])
    tot = ss[0]
    for o in range(1, NSEC):
        tot = tot + ss[o]
    inv_row = lax.rsqrt(tot / D + EPSILON)
    inv = jnp.broadcast_to(inv_row, (128, TOK)).T
    for t in range(5):
        cols = slice(t * 128, (t + 1) * 128)
        n_t = (h_v[:, cols].astype(F32) * inv * gain_v[:, cols]).astype(BF16)
        ngat[core, zz, :, cols] = n_t

    my_rows = pl.ds(pl.multiple_of(yy * RB, RB), RB)

    def scatter(j, part, rs, s, r):
        for o in range(1, NSEC):
            d = sec_peer[o]
            rcopy(
                part.at[j, lax.rem(d, 2), pl.ds(pl.multiple_of(lax.div(d, 2) * RB, RB), RB), :],
                rs.at[j, o - 1], s.at[j], r.at[j], sec_dev[o],
            ).start()
        send_total(rs.at[j], s.at[j])

    def reduce_and_gather(j, part, rs, rs_r, st, dst, s, r):
        wait_bytes(rs.at[j], rs_r.at[j])
        tot = part[j, xl, my_rows, :]
        for o in range(1, NSEC):
            tot = tot + rs[j, o - 1]
        st[j] = tot.astype(BF16)
        piece = dst.at[j, xl, my_rows, :]
        for o in range(1, NSEC):
            rcopy(st.at[j], piece, s.at[j], r.at[j], sec_dev[o]).start()
        pltpu.make_async_copy(st.at[j], piece, r.at[j]).start()
        send_total(rs.at[j, :, 0:RB // 2, :], s.at[j])

    def weight_cols(j):
        return jnp.concatenate(
            [w_v[:, j * 128:(j + 1) * 128], w_v[:, 512 + j * 128:512 + (j + 1) * 128]], axis=1
        )

    def do_s(j):
        pj = dot(ngat[core, zz], weight_cols(j))
        part_a[j, 0] = pj[:, 0:128]
        part_a[j, 1] = pj[:, 128:256]
        scatter(j, part_a, rs_a, ra_s, ra_r)

    for j in range(AHEAD):
        do_s(j)
    def ring(j, d):
        sign = 1 if d == 0 else -1
        hops = 4 if (j + d) % 2 == 0 else 3
        slot0 = 0 if d == 0 else (3 if j % 2 else 4)
        return sign, hops, slot0

    ng_c = {}

    def do_ng(s, h):
        rows = pl.ds(h * 96, 96)
        if s == 0:
            own = ngat.at[core, zz, rows]
            rcopy(own, own, nc_s.at[0], nc_r.at[0], core_dev).start()
        for d in range(2):
            sign, hops, slot0 = ring(h, d)
            piece = ngat.at[core, z_at[(-sign * s) % NZ], rows]
            if 0 < s <= hops:
                ng_c[h, d, s - 1].wait_recv()
            if s < hops:
                c = rcopy(piece, piece, ng_s.at[0], ng_r.at[h, slot0 + s], z_dev[sign % NZ])
                c.start()
                ng_c[h, d, s] = c
            if 0 < s <= hops:
                rcopy(piece, piece, nc_s.at[0], nc_r.at[0], core_dev).start()

    do_ng(0, 0)
    do_ng(0, 1)
    send_total(ngat.at[0, 1:NZ], ng_s.at[0])
    send_total(ngat.at[0], nc_s.at[0])
    loads[3].wait()
    loads[4].wait()

    def do_r(j):
        reduce_and_gather(j, part_a, rs_a, ra_r, st_a, kvb, aa_s, aa_r)

    mask_a = (
        lax.broadcasted_iota(jnp.int32, (128, 128), 0)
        <= lax.broadcasted_iota(jnp.int32, (128, 128), 1)
    )
    qpos = lax.broadcasted_iota(jnp.int32, (64, 128), 1)
    mask_b = lax.broadcasted_iota(jnp.int32, (64, 128), 0) <= jnp.where(qpos < 64, qpos, qpos - 64)

    def soft(s, dpr):
        m = jnp.max(s, axis=0, keepdims=True)
        e = jnp.exp(s - m)
        p = e * (1.0 / jnp.sum(e, axis=0, keepdims=True))
        inner = jnp.sum(p * dpr, axis=0, keepdims=True)
        return p.astype(BF16), (p * (dpr - inner)).astype(BF16)

    def do_t(j):
        wait_bytes(kvb.at[j], aa_r.at[j])
        k = kvb[j, 0]
        v = kvb[j, 1]
        k_lo = k[0:128]
        v_lo = v[0:128]
        col0 = j * GRP * HD

        def heads(ref, rows, hs):
            return [ref[rows, col0 + h * HD:col0 + (h + 1) * HD] for h in hs]

        lo, hi = slice(0, 128), slice(128, TOK)
        for h in range(GRP):
            qh = heads(q_v, lo, [h])[0]
            gh = heads(g_v, lo, [h])[0]
            s = jnp.where(mask_a, dot(k_lo, qh, NT) * SCALE, -1e30)
            p, ds = soft(s, dot(v_lo, gh, NT))
            pbuf_a[:, h * 128:(h + 1) * 128] = p
            dsbuf_a[:, h * 128:(h + 1) * 128] = ds
        q_hi = jnp.concatenate(heads(q_v, hi, range(GRP)) + heads(q_v, hi, [GRP - 1]), axis=0)
        g_hi = jnp.concatenate(heads(g_v, hi, range(GRP)) + heads(g_v, hi, [GRP - 1]), axis=0)
        for i in range(3):
            qh = q_hi[i * 128:(i + 1) * 128]
            gh = g_hi[i * 128:(i + 1) * 128]
            s = dot(k, qh, NT) * SCALE
            s = jnp.concatenate([s[0:128], jnp.where(mask_b, s[128:TOK], -1e30)], axis=0)
            p, ds = soft(s, dot(v, gh, NT))
            pbuf_b[:, i * 128:(i + 1) * 128] = p
            dsbuf_b[:, i * 128:(i + 1) * 128] = ds
        q_lo = jnp.concatenate(heads(q_v, lo, range(GRP)), axis=0)
        g_lo = jnp.concatenate(heads(g_v, lo, range(GRP)), axis=0)
        nb = 64 * GRP
        kb = dot(dsbuf_b[:, 0:nb], q_hi[0:nb])
        vb = dot(pbuf_b[:, 0:nb], g_hi[0:nb])
        ka = dot(dsbuf_a[...], q_lo)
        va = dot(pbuf_a[...], g_lo)
        part_b[j, 0, 0:128] = (ka + kb[0:128]) * SCALE
        part_b[j, 0, 128:TOK] = kb[128:TOK] * SCALE
        part_b[j, 1, 0:128] = va + vb[0:128]
        part_b[j, 1, 128:TOK] = vb[128:TOK]
        scatter(j, part_b, rs_b, rb_s, rb_r)
        qa = dot(dsbuf_a[...], k_lo, TN) * SCALE
        qb = dot(dsbuf_b[:, 0:nb], k, TN) * SCALE
        for h in range(GRP):
            qg_v[0:128, col0 + h * HD:col0 + (h + 1) * HD] = qa[h * 128:(h + 1) * 128].astype(BF16)
            qg_v[128:TOK, col0 + h * HD:col0 + (h + 1) * HD] = qb[h * 64:(h + 1) * 64].astype(BF16)

    def do_u(j):
        reduce_and_gather(j, part_b, rs_b, rb_r, st_b, kvg, ab_s, ab_r)

    def do_x(j):
        wait_bytes(kvg.at[j], ab_r.at[j])
        for kv in range(2):
            turned = kvg[j, kv].T
            for z in range(NZ):
                kvt[j, kv, z] = turned[z * 16:(z + 1) * 16]
        slot = kvr.at[j, core, zz]
        for o in range(1, NZ):
            rcopy(kvt.at[j, core, z_at[o]], slot, kt_s.at[j], kt_r.at[j], z_dev[o]).start()
        for o in range(NZ):
            rcopy(kvt.at[j, 1 - core, z_at[o]], slot, ku_s.at[j], kt_r.at[j], z_dev2[o]).start()
        pltpu.make_async_copy(kvt.at[j, core, zz], slot, kt_r.at[j]).start()
        send_total(kvr.at[j, 0, 1:NZ], kt_s.at[j])
        send_total(kvr.at[j, 0], ku_s.at[j])

    x_c = {}

    def do_k(j):
        if j == 0:
            wait_bytes(ngat.at[0], nc_r.at[0])
        wait_bytes(kvr.at[j], kt_r.at[j])
        tot = None
        for c in range(2):
            for z in range(NZ):
                term = dot(kvr[j, c, z], ngat[c, z])
                tot = term if tot is None else tot + term
        xs[j] = tot
        c = rcopy(xs.at[j], xr.at[j], x_s.at[j], x_r.at[j], x_dev)
        start(c)
        x_c[j] = c

    def do_nf(j):
        both = jnp.concatenate([kvg[j, 0], kvg[j, 1]], axis=1)
        term = dot(both, weight_cols(j), NT)
        nf[...] = term if j == 0 else nf[...] + term

    def do_gain():
        gpair[0] = jnp.zeros((8, 128), F32)
        for t in range(5):
            cols = slice(t * 128, (t + 1) * 128)
            full = nf[:, cols]
            ng_v[:, cols] = full.astype(BF16)
            term = full * h_v[:, cols].astype(F32) * inv
            gpair[0, t:t + 1, :] = jnp.sum(term, axis=0, keepdims=True)
        c = rcopy(gpair.at[0], gpair.at[1], gp_s.at[0], gp_r.at[0], core_dev)
        start(c)
        g_c["p"] = c

    g_c = {}

    def do_gain_z():
        g_c["p"].wait_recv()
        gz[zz] = gpair[0] + gpair[1]
        for o in range(1, NZ):
            rcopy(gz.at[zz], gz.at[zz], gz_s.at[0], gz_r.at[0], z_dev[o]).start()
        send_total(gz.at[1:NZ], gz_s.at[0])

    def do_gain_x():
        wait_bytes(gz.at[1:NZ], gz_r.at[0])
        tot = gz[0]
        for i in range(1, NZ):
            tot = tot + gz[i]
        gpair[2] = tot
        c = rcopy(gpair.at[2], gpair.at[3], gx_s.at[0], gx_r.at[0], x_dev)
        start(c)
        g_c["x"] = c

    def do_gain_end():
        g_c["x"].wait_recv()
        gx[...] = (gpair[2] + gpair[3]) * (1.0 / 32.0)

    az_c = {}

    def do_g(j):
        x_c[j].wait_recv()
        wgb[core, j, zz] = ((xs[j] + xr[j]) * (1.0 / 32.0)).astype(BF16)
        if j in DIRECT:
            piece = wgb.at[core, j, zz]
            for o in range(1, NZ):
                rcopy(piece, piece, az_s.at[j], az_r.at[j, 0], z_dev[o]).start()
        else:
            do_a(j, 0)
        send_total(wgb.at[0, j, 1:NZ], az_s.at[j])

    def do_a(j, s):
        for d in range(2):
            sign, hops, slot0 = ring(j, d)
            if 0 < s <= hops:
                az_c[j, d, s - 1].wait_recv()
            if s < hops:
                chunk = z_at[(-sign * s) % NZ]
                piece = wgb.at[core, j, chunk]
                c = rcopy(piece, piece, az_s.at[j], az_r.at[j, slot0 + s], z_dev[sign % NZ])
                c.start()
                az_c[j, d, s] = c

    cc_c = {}

    def do_cc(j):
        if j in DIRECT:
            wait_bytes(wgb.at[0, j, 1:NZ], az_r.at[j, 0])
        piece = wgb.at[core, j]
        c = rcopy(piece, piece, cc_s.at[j], cc_r.at[j], core_dev)
        start(c)
        cc_c[j] = c

    def do_out(j):
        cc_c[j].wait_recv()
        for half in range(2):
            wide = wgb[half, j].astype(F32).reshape(128, FEAT)
            wg_v[:, half * 512 + j * 128:half * 512 + (j + 1) * 128] = wide.T

    R, T, U, X, N, H = do_r, do_t, do_u, do_x, do_nf, do_ng
    K, G, A, C, O = do_k, do_g, do_a, do_cc, do_out
    steps = [
        (R, 0), (H, 1, 0), (R, 1), (H, 1, 1), (R, 2), (H, 2, 0), (R, 3), (T, 0), (H, 2, 1), (T, 1), (T, 2),
        (H, 3, 0), (T, 3), (H, 3, 1), (U, 0), (U, 1), (H, 4, 0), (U, 2), (U, 3), (H, 4, 1),
        (X, 0), (X, 1), (X, 2), (X, 3), (N, 0), (N, 1), (N, 2), (N, 3),
        (do_gain,), (K, 0), (do_gain_z,), (K, 1), (G, 0), (K, 2), (G, 1), (K, 3), (do_gain_x,),
        (G, 2), (G, 3), (C, 0), (C, 1), (O, 0), (do_gain_end,), (C, 2), (O, 1), (C, 3), (O, 2), (O, 3),
    ]
    for step in steps:
        step[0](*step[1:])

    for wait in sends:
        wait()


def finish_kernel(qg, wg, gx, ng, qg_out, wg_out, gg_out, ng_out, sem):
    copies = [(wg.at[i * 80:(i + 1) * 80], wg_out.at[i * 80:(i + 1) * 80]) for i in range(8)]
    copies += [(qg.at[i * 48:(i + 1) * 48], qg_out.at[i * 48:(i + 1) * 48]) for i in range(4)]
    copies += [(ng, ng_out)]
    copies += [(gx.at[t], gg_out.at[t * 128:(t + 1) * 128]) for t in range(5)]
    copies = [pltpu.make_async_copy(a, b, sem.at[i]) for i, (a, b) in enumerate(copies)]
    for c in copies:
        c.start()
    for c in copies:
        c.wait()


def shards(hidden, norm_gain, kv_weight, queries, out_grad):
    hbm = pl.BlockSpec(memory_space=pltpu.HBM)
    in_vmem = pl.BlockSpec(memory_space=pltpu.VMEM)
    dma = pltpu.SemaphoreType.DMA
    vm = pltpu.VMEM
    scratch = [
        vm((TOK, FEAT), BF16), vm((1, FEAT), F32), vm((FEAT, 1024), BF16),
        vm((TOK, QH * HD), BF16), vm((TOK, QH * HD), BF16),
        vm((NSEC, 1, TOK), F32), vm((2, NZ, TOK, FEAT), BF16),
        vm((KVH, 2, TOK, HD), F32), vm((KVH, 7, RB, HD), F32), vm((KVH, RB, HD), BF16),
        vm((KVH, 2, TOK, HD), BF16),
        vm((KVH, 2, TOK, HD), F32), vm((KVH, 7, RB, HD), F32), vm((KVH, RB, HD), BF16),
        vm((KVH, 2, TOK, HD), BF16), vm((KVH, 2, NZ, 16, TOK), BF16), vm((KVH, 2, NZ, 16, TOK), BF16),
        vm((128, 640), BF16), vm((128, 640), BF16), vm((TOK, 384), BF16), vm((TOK, 384), BF16),
        vm((TOK, FEAT), F32),
        vm((KVH, 16, FEAT), F32), vm((KVH, 16, FEAT), F32), vm((2, KVH, NZ, 16, FEAT), BF16),
        vm((4, 8, 128), F32), vm((NZ, 8, 128), F32),
        dma((5,)), dma((1,)), dma((1,)), dma((1,)), dma((2, 7)), dma((1,)), dma((1,)),
        dma((KVH,)), dma((KVH,)), dma((KVH,)), dma((KVH,)),
        dma((KVH,)), dma((KVH,)), dma((KVH,)), dma((KVH,)),
        dma((KVH,)), dma((KVH,)), dma((KVH,)), dma((KVH,)), dma((KVH,)),
        dma((KVH,)), dma((KVH, 7)), dma((KVH,)), dma((KVH,)),
        dma((1,)), dma((1,)), dma((1,)), dma((1,)), dma((1,)), dma((1,)),
    ]
    held = pl.pallas_call(
        fused_kernel,
        out_shape=(
            vm((TOK, QH * HD), BF16),
            vm((FEAT, 1024), F32),
            vm((8, 128), F32),
            vm((TOK, FEAT), BF16),
        ),
        in_specs=[hbm] * 5,
        out_specs=(in_vmem,) * 4,
        scratch_shapes=scratch,
        compiler_params=pltpu.CompilerParams(
            collective_id=0, has_side_effects=True, vmem_limit_bytes=40 * 1024 * 1024
        ),
        name="fused",
    )(*[pltpu.with_memory_space_constraint(a, pltpu.HBM) for a in (hidden, norm_gain, kv_weight, queries, out_grad)])
    query_grad, weight_grad, gain_grad, normed_grad = pl.pallas_call(
        finish_kernel,
        out_shape=(
            jax.ShapeDtypeStruct((TOK, QH * HD), BF16),
            jax.ShapeDtypeStruct((FEAT, 1024), F32),
            jax.ShapeDtypeStruct((FEAT,), F32),
            jax.ShapeDtypeStruct((TOK, FEAT), BF16),
        ),
        in_specs=[in_vmem] * 4,
        out_specs=(hbm,) * 4,
        scratch_shapes=[dma((18,))],
        compiler_params=pltpu.CompilerParams(vmem_limit_bytes=1024 * 1024),
        name="finish",
    )(*[pltpu.with_memory_space_constraint(a, pltpu.VMEM) for a in held])
    return query_grad, weight_grad, gain_grad, normed_grad


def solution(mesh):
    placed = (
        P("dp", "section"),
        P("section"),
        P("section", None),
        P("dp", "section"),
        P("dp", "section"),
    )
    return jax.shard_map(
        shards,
        mesh=mesh,
        in_specs=placed,
        out_specs=(P("dp", "section"), P("section", None), P("section"), P("dp", "section")),
        check_vma=False,
    )
```

time: 102 us -> 74.6 us (0.73)
  Pallas kernels: 92.8 us -> 73.9 us
  local copies, waits for them, and re-layouts: 8.64 us -> 0 us
    pallas_call x2, Pallas kernels: 92.8 us -> 73.9 us  [the longest x1 71.8 us: shards(): pl.pallas_call(fused_kernel, out_shape=(vm((TOK, QH * HD), BF16), vm((FEA...]
    unnamed x12 -> x0, local copies, waits for them, and re-layouts: 7.36 us -> none
    reshape x2 -> x0, local copies, waits for them, and re-layouts: 1.28 us -> none  [the longest x1 0.69 us: shards(): norm_gain.reshape(1, FEAT)]
where the time goes in v2:
time: 74.6 us; the launch traced here: 74.5 us
  Pallas kernels  73.9 us (99%)
    pallas_call x1, Pallas kernels, shards(): pl.pallas_call(fused_kernel, out_shape=(vm((TOK, QH * HD), BF16), vm((FEA...  71.8 us
    pallas_call x1, Pallas kernels, shards(): pl.pallas_call(finish_kernel, out_shape=(jax.ShapeDtypeStruct((TOK, QH *...  2.05 us

profile of v2, /device:TPU:1, one launch (start us, length us, event | category | flops | bytes accessed | tf_op | source)
XLA Modules:
  0.0 74.5 jit_solution(10661113068052036538)
XLA Ops:
  0.6 71.8 %fused.1 = (bf16[192,2560]{1,0:T(8,128)(2,1)S(1)}, f32[640,1024]{1,0:T(8,128)S(1)}, f32[8,128]{1,0:T(8,128)S(1)}, bf16[192,640]{1,0:T(8,128)(2,1)S(1)}) custom-call(bf16[192,640]{1,0:T(8,128)(2,1)} %h_hbm.1, f32[640]{0:T(1024)} %gain_hbm.1, bf16[640,1024]{1,0:T(8,128)(2,1)} %w_hbm.1, bf16[192,2560]{1,0:T(8,128)(2,1)} %q_hbm.1, bf16[192,2560]{1,0:T(8,128)(2,1)} %g_hbm.1), custom_call_target="tpu_custom_call" | custom-call | tf_op jit(solution)/shard_map/fused/pallas_call | solution.py:421
  72.4 2.0 %finish.1 = (bf16[192,2560]{1,0:T(8,128)(2,1)}, f32[640,1024]{1,0:T(8,128)}, f32[640]{0:T(1024)}, bf16[192,640]{1,0:T(8,128)(2,1)}) custom-call(bf16[192,2560]{1,0:T(8,128)(2,1)S(1)} %get-tuple-element.8.qg, f32[640,1024]{1,0:T(8,128)S(1)} %get-tuple-element.9.wg, f32[8,128]{1,0:T(8,128)S(1)} %get-tuple-element.10.gx, bf16[192,640]{1,0:T(8,128)(2,1)S(1)} %get-tuple-element.11.ng), custom_call_target="tpu_custom_call" | custom-call | tf_op jit(solution)/shard_map/finish/pallas_call | solution.py:437

commit v3 on v2

--- a/solution.py
+++ b/solution.py
@@ -16,8 +16,7 @@
 FEAT = 640
 HALF = FEAT // 2
 RB = 48
-AHEAD = 4
-DIRECT = (0, 1, 2, 3)
+AHEAD = 3
 EPSILON = 1e-05
 SCALE = HD ** (-0.5)
 MESH = pl.DeviceIdType.MESH
@@ -325,36 +324,27 @@
         g_c["x"].wait_recv()
         gx[...] = (gpair[2] + gpair[3]) * (1.0 / 32.0)
 
-    az_c = {}
-
     def do_g(j):
         x_c[j].wait_recv()
         wgb[core, j, zz] = ((xs[j] + xr[j]) * (1.0 / 32.0)).astype(BF16)
-        if j in DIRECT:
-            piece = wgb.at[core, j, zz]
-            for o in range(1, NZ):
-                rcopy(piece, piece, az_s.at[j], az_r.at[j, 0], z_dev[o]).start()
-        else:
-            do_a(j, 0)
+        piece = wgb.at[core, j, zz]
+        for o, slot in ((2, 0), (NZ - 2, 1), (1, 2), (NZ - 1, 2)):
+            rcopy(piece, piece, az_s.at[j], az_r.at[j, slot], z_dev[o]).start()
         send_total(wgb.at[0, j, 1:NZ], az_s.at[j])
 
-    def do_a(j, s):
-        for d in range(2):
-            sign, hops, slot0 = ring(j, d)
-            if 0 < s <= hops:
-                az_c[j, d, s - 1].wait_recv()
-            if s < hops:
-                chunk = z_at[(-sign * s) % NZ]
-                piece = wgb.at[core, j, chunk]
-                c = rcopy(piece, piece, az_s.at[j], az_r.at[j, slot0 + s], z_dev[sign % NZ])
-                c.start()
-                az_c[j, d, s] = c
+    def do_a(j):
+        for slot in range(2):
+            sign = 1 - 2 * slot
+            piece = wgb.at[core, j, z_at[(-2 * sign) % NZ]]
+            wait_bytes(piece, az_r.at[j, slot])
+            far = [2 * sign] if j % 2 == slot else []
+            for o in far + [sign]:
+                rcopy(piece, piece, az_s.at[j], az_r.at[j, 2], z_dev[o % NZ]).start()
 
     cc_c = {}
 
     def do_cc(j):
-        if j in DIRECT:
-            wait_bytes(wgb.at[0, j, 1:NZ], az_r.at[j, 0])
+        wait_bytes(wgb.at[0, j, 0:5], az_r.at[j, 2])
         piece = wgb.at[core, j]
         c = rcopy(piece, piece, cc_s.at[j], cc_r.at[j], core_dev)
         start(c)
@@ -366,14 +356,15 @@
             wide = wgb[half, j].astype(F32).reshape(128, FEAT)
             wg_v[:, half * 512 + j * 128:half * 512 + (j + 1) * 128] = wide.T
 
-    R, T, U, X, N, H = do_r, do_t, do_u, do_x, do_nf, do_ng
+    S, R, T, U, X, N, H = do_s, do_r, do_t, do_u, do_x, do_nf, do_ng
     K, G, A, C, O = do_k, do_g, do_a, do_cc, do_out
     steps = [
-        (R, 0), (H, 1, 0), (R, 1), (H, 1, 1), (R, 2), (H, 2, 0), (R, 3), (T, 0), (H, 2, 1), (T, 1), (T, 2),
-        (H, 3, 0), (T, 3), (H, 3, 1), (U, 0), (U, 1), (H, 4, 0), (U, 2), (U, 3), (H, 4, 1),
-        (X, 0), (X, 1), (X, 2), (X, 3), (N, 0), (N, 1), (N, 2), (N, 3),
-        (do_gain,), (K, 0), (do_gain_z,), (K, 1), (G, 0), (K, 2), (G, 1), (K, 3), (do_gain_x,),
-        (G, 2), (G, 3), (C, 0), (C, 1), (O, 0), (do_gain_end,), (C, 2), (O, 1), (C, 3), (O, 2), (O, 3),
+        (R, 0), (S, 3), (H, 1, 0), (R, 1), (H, 1, 1), (R, 2), (T, 0), (H, 2, 0), (R, 3), (T, 1),
+        (H, 2, 1), (H, 3, 0), (U, 0), (T, 2), (H, 3, 1), (T, 3), (H, 4, 0), (X, 0), (U, 1), (U, 2),
+        (H, 4, 1), (U, 3), (X, 1), (X, 2), (X, 3), (N, 0), (N, 1), (N, 2), (N, 3), (do_gain,),
+        (K, 0), (do_gain_z,), (K, 1), (K, 2), (G, 0), (K, 3), (do_gain_x,), (G, 1), (A, 0), (G, 2),
+        (A, 1), (G, 3), (A, 2), (C, 0), (A, 3), (C, 1), (O, 0), (do_gain_end,), (C, 2), (O, 1),
+        (C, 3), (O, 2), (O, 3),
     ]
     for step in steps:
         step[0](*step[1:])
@@ -415,7 +406,7 @@
         dma((KVH,)), dma((KVH,)), dma((KVH,)), dma((KVH,)),
         dma((KVH,)), dma((KVH,)), dma((KVH,)), dma((KVH,)),
         dma((KVH,)), dma((KVH,)), dma((KVH,)), dma((KVH,)), dma((KVH,)),
-        dma((KVH,)), dma((KVH, 7)), dma((KVH,)), dma((KVH,)),
+        dma((KVH,)), dma((KVH, 3)), dma((KVH,)), dma((KVH,)),
         dma((1,)), dma((1,)), dma((1,)), dma((1,)), dma((1,)), dma((1,)),
     ]
     held = pl.pallas_call(

time: 74.6 us -> 70.9 us (0.950)
  Pallas kernels: 73.9 us -> 69.9 us
    pallas_call x1, Pallas kernels: 71.8 us -> 67.9 us  [shards(): pl.pallas_call(fused_kernel, out_shape=(vm((TOK, QH * HD), BF16), vm((FEA...]
where the time goes in v3:
time: 70.9 us; the launch traced here: 70.6 us
  Pallas kernels  69.9 us (99%)
    pallas_call x1, Pallas kernels, shards(): pl.pallas_call(fused_kernel, out_shape=(vm((TOK, QH * HD), BF16), vm((FEA...  67.9 us
    pallas_call x1, Pallas kernels, shards(): pl.pallas_call(finish_kernel, out_shape=(jax.ShapeDtypeStruct((TOK, QH *...  2.05 us

profile of v3, /device:TPU:1, one launch (start us, length us, event | category | flops | bytes accessed | tf_op | source)
XLA Modules:
  0.0 70.6 jit_solution(1672430789846664053)
XLA Ops:
  0.6 67.9 %fused.1 = (bf16[192,2560]{1,0:T(8,128)(2,1)S(1)}, f32[640,1024]{1,0:T(8,128)S(1)}, f32[8,128]{1,0:T(8,128)S(1)}, bf16[192,640]{1,0:T(8,128)(2,1)S(1)}) custom-call(bf16[192,640]{1,0:T(8,128)(2,1)} %h_hbm.1, f32[640]{0:T(1024)} %gain_hbm.1, bf16[640,1024]{1,0:T(8,128)(2,1)} %w_hbm.1, bf16[192,2560]{1,0:T(8,128)(2,1)} %q_hbm.1, bf16[192,2560]{1,0:T(8,128)(2,1)} %g_hbm.1), custom_call_target="tpu_custom_call" | custom-call | tf_op jit(solution)/shard_map/fused/pallas_call | solution.py:412
  68.5 2.0 %finish.1 = (bf16[192,2560]{1,0:T(8,128)(2,1)}, f32[640,1024]{1,0:T(8,128)}, f32[640]{0:T(1024)}, bf16[192,640]{1,0:T(8,128)(2,1)}) custom-call(bf16[192,2560]{1,0:T(8,128)(2,1)S(1)} %get-tuple-element.8.qg, f32[640,1024]{1,0:T(8,128)S(1)} %get-tuple-element.9.wg, f32[8,128]{1,0:T(8,128)S(1)} %get-tuple-element.10.gx, bf16[192,640]{1,0:T(8,128)(2,1)S(1)} %get-tuple-element.11.ng), custom_call_target="tpu_custom_call" | custom-call | tf_op jit(solution)/shard_map/finish/pallas_call | solution.py:428

commit v4 on v3

--- a/solution.py
+++ b/solution.py
@@ -360,10 +360,10 @@
     K, G, A, C, O = do_k, do_g, do_a, do_cc, do_out
     steps = [
         (R, 0), (S, 3), (H, 1, 0), (R, 1), (H, 1, 1), (R, 2), (T, 0), (H, 2, 0), (R, 3), (T, 1),
-        (H, 2, 1), (H, 3, 0), (U, 0), (T, 2), (H, 3, 1), (T, 3), (H, 4, 0), (X, 0), (U, 1), (U, 2),
-        (H, 4, 1), (U, 3), (X, 1), (X, 2), (X, 3), (N, 0), (N, 1), (N, 2), (N, 3), (do_gain,),
-        (K, 0), (do_gain_z,), (K, 1), (K, 2), (G, 0), (K, 3), (do_gain_x,), (G, 1), (A, 0), (G, 2),
-        (A, 1), (G, 3), (A, 2), (C, 0), (A, 3), (C, 1), (O, 0), (do_gain_end,), (C, 2), (O, 1),
+        (H, 2, 1), (T, 2), (H, 3, 0), (U, 0), (T, 3), (H, 3, 1), (U, 1), (H, 4, 0), (X, 0), (U, 2),
+        (U, 3), (H, 4, 1), (X, 1), (X, 2), (X, 3), (K, 0), (K, 1), (N, 0), (N, 1), (N, 2),
+        (N, 3), (do_gain,), (K, 2), (G, 0), (do_gain_z,), (K, 3), (G, 1), (G, 2), (A, 0), (G, 3),
+        (A, 1), (do_gain_x,), (A, 2), (C, 0), (A, 3), (C, 1), (O, 0), (C, 2), (O, 1), (do_gain_end,),
         (C, 3), (O, 2), (O, 3),
     ]
     for step in steps:

time: 70.9 us -> 69.8 us (0.984)
  Pallas kernels: 69.9 us -> 69.1 us
    pallas_call x1, Pallas kernels: 67.9 us -> 67 us  [shards(): pl.pallas_call(fused_kernel, out_shape=(vm((TOK, QH * HD), BF16), vm((FEA...]
where the time goes in v4:
time: 69.8 us; the launch traced here: 69.7 us
  Pallas kernels  69.1 us (99%)
    pallas_call x1, Pallas kernels, shards(): pl.pallas_call(fused_kernel, out_shape=(vm((TOK, QH * HD), BF16), vm((FEA...  67 us
    pallas_call x1, Pallas kernels, shards(): pl.pallas_call(finish_kernel, out_shape=(jax.ShapeDtypeStruct((TOK, QH *...  2.05 us

profile of v4, /device:TPU:1, one launch (start us, length us, event | category | flops | bytes accessed | tf_op | source)
XLA Modules:
  0.0 69.7 jit_solution(1548810292087113929)
XLA Ops:
  0.6 67.0 %fused.1 = (bf16[192,2560]{1,0:T(8,128)(2,1)S(1)}, f32[640,1024]{1,0:T(8,128)S(1)}, f32[8,128]{1,0:T(8,128)S(1)}, bf16[192,640]{1,0:T(8,128)(2,1)S(1)}) custom-call(bf16[192,640]{1,0:T(8,128)(2,1)} %h_hbm.1, f32[640]{0:T(1024)} %gain_hbm.1, bf16[640,1024]{1,0:T(8,128)(2,1)} %w_hbm.1, bf16[192,2560]{1,0:T(8,128)(2,1)} %q_hbm.1, bf16[192,2560]{1,0:T(8,128)(2,1)} %g_hbm.1), custom_call_target="tpu_custom_call" | custom-call | tf_op jit(solution)/shard_map/fused/pallas_call | solution.py:412
  67.7 2.0 %finish.1 = (bf16[192,2560]{1,0:T(8,128)(2,1)}, f32[640,1024]{1,0:T(8,128)}, f32[640]{0:T(1024)}, bf16[192,640]{1,0:T(8,128)(2,1)}) custom-call(bf16[192,2560]{1,0:T(8,128)(2,1)S(1)} %get-tuple-element.8.qg, f32[640,1024]{1,0:T(8,128)S(1)} %get-tuple-element.9.wg, f32[8,128]{1,0:T(8,128)S(1)} %get-tuple-element.10.gx, bf16[192,640]{1,0:T(8,128)(2,1)S(1)} %get-tuple-element.11.ng), custom_call_target="tpu_custom_call" | custom-call | tf_op jit(solution)/shard_map/finish/pallas_call | solution.py:428

commit v5 on v4

--- a/solution.py
+++ b/solution.py
@@ -17,6 +17,8 @@
 HALF = FEAT // 2
 RB = 48
 AHEAD = 3
+SEC_FAR = (3, 5, 4, 1, 7, 2, 6)
+Z_FAR = (4, 3, 5, 2, 6, 1, 7)
 EPSILON = 1e-05
 SCALE = HD ** (-0.5)
 MESH = pl.DeviceIdType.MESH
@@ -102,7 +104,7 @@
     row = jnp.sum(acc.T, axis=0, keepdims=True)
     ss[0] = row
     pl.semaphore_wait(bar, len(partners))
-    for o in range(1, NSEC):
+    for o in SEC_FAR:
         rcopy(ss.at[0], ss.at[o], ss_s.at[0], ss_r.at[0], sec_dev[o]).start()
     send_total(ss.at[1:NSEC], ss_s.at[0])
     loads[1].wait()
@@ -121,7 +123,7 @@
     my_rows = pl.ds(pl.multiple_of(yy * RB, RB), RB)
 
     def scatter(j, part, rs, s, r):
-        for o in range(1, NSEC):
+        for o in SEC_FAR:
             d = sec_peer[o]
             rcopy(
                 part.at[j, lax.rem(d, 2), pl.ds(pl.multiple_of(lax.div(d, 2) * RB, RB), RB), :],
@@ -136,7 +138,7 @@
             tot = tot + rs[j, o - 1]
         st[j] = tot.astype(BF16)
         piece = dst.at[j, xl, my_rows, :]
-        for o in range(1, NSEC):
+        for o in SEC_FAR:
             rcopy(st.at[j], piece, s.at[j], r.at[j], sec_dev[o]).start()
         pltpu.make_async_copy(st.at[j], piece, r.at[j]).start()
         send_total(rs.at[j, :, 0:RB // 2, :], s.at[j])
@@ -260,10 +262,10 @@
             for z in range(NZ):
                 kvt[j, kv, z] = turned[z * 16:(z + 1) * 16]
         slot = kvr.at[j, core, zz]
-        for o in range(1, NZ):
+        for o in Z_FAR:
             rcopy(kvt.at[j, core, z_at[o]], slot, kt_s.at[j], kt_r.at[j], z_dev[o]).start()
-        for o in range(NZ):
             rcopy(kvt.at[j, 1 - core, z_at[o]], slot, ku_s.at[j], kt_r.at[j], z_dev2[o]).start()
+        rcopy(kvt.at[j, 1 - core, zz], slot, ku_s.at[j], kt_r.at[j], core_dev).start()
         pltpu.make_async_copy(kvt.at[j, core, zz], slot, kt_r.at[j]).start()
         send_total(kvr.at[j, 0, 1:NZ], kt_s.at[j])
         send_total(kvr.at[j, 0], ku_s.at[j])

time: 69.8 us -> 69.6 us (level)
  no operation moved by 1% of the time
where the time goes in v5:
time: 69.6 us; the launch traced here: 69.5 us
  Pallas kernels  68.8 us (99%)
    pallas_call x1, Pallas kernels, shards(): pl.pallas_call(fused_kernel, out_shape=(vm((TOK, QH * HD), BF16), vm((FEA...  66.8 us
    pallas_call x1, Pallas kernels, shards(): pl.pallas_call(finish_kernel, out_shape=(jax.ShapeDtypeStruct((TOK, QH *...  2.05 us

profile of v5, /device:TPU:1, one launch (start us, length us, event | category | flops | bytes accessed | tf_op | source)
XLA Modules:
  0.0 69.5 jit_solution(13202502152759388382)
XLA Ops:
  0.6 66.8 %fused.1 = (bf16[192,2560]{1,0:T(8,128)(2,1)S(1)}, f32[640,1024]{1,0:T(8,128)S(1)}, f32[8,128]{1,0:T(8,128)S(1)}, bf16[192,640]{1,0:T(8,128)(2,1)S(1)}) custom-call(bf16[192,640]{1,0:T(8,128)(2,1)} %h_hbm.1, f32[640]{0:T(1024)} %gain_hbm.1, bf16[640,1024]{1,0:T(8,128)(2,1)} %w_hbm.1, bf16[192,2560]{1,0:T(8,128)(2,1)} %q_hbm.1, bf16[192,2560]{1,0:T(8,128)(2,1)} %g_hbm.1), custom_call_target="tpu_custom_call" | custom-call | tf_op jit(solution)/shard_map/fused/pallas_call | solution.py:414
  67.4 2.0 %finish.1 = (bf16[192,2560]{1,0:T(8,128)(2,1)}, f32[640,1024]{1,0:T(8,128)}, f32[640]{0:T(1024)}, bf16[192,640]{1,0:T(8,128)(2,1)}) custom-call(bf16[192,2560]{1,0:T(8,128)(2,1)S(1)} %get-tuple-element.8.qg, f32[640,1024]{1,0:T(8,128)S(1)} %get-tuple-element.9.wg, f32[8,128]{1,0:T(8,128)S(1)} %get-tuple-element.10.gx, bf16[192,640]{1,0:T(8,128)(2,1)S(1)} %get-tuple-element.11.ng), custom_call_target="tpu_custom_call" | custom-call | tf_op jit(solution)/shard_map/finish/pallas_call | solution.py:430
